TPU v7x, 256 devices: a whole 4x4x8 slice. The times are simulated.
256 devices in a mesh: segment: 4 (over y_hi, core), ctx: 64 (over x, z, y_lo).
Axes of the slice: x: 4, y: 4 (y_hi: 2, y_lo: 2; y = y_hi * 2 + y_lo), z: 8, core: 2. Of those that a mesh axis runs over, the one named last changes fastest.
Arguments:
- saved_inputs: bfloat16 [4, 2, 8192, 2048], P('segment', None, 'ctx'), may hold values from -6 to 6
- scale_gains: float32 [4, 3, 2048], P('segment'), may hold values from 0.1 to 1.9
- out_proj: bfloat16 [4, 2048, 2048], P('segment'), may hold values from -0.125 to 0.125
- top_grad: bfloat16 [2, 8192, 2048], P(None, 'ctx'), may hold values from -6 to 6
Outputs:
- input_grads: bfloat16 [4, 2, 8192, 2048], P('segment', None, 'ctx')
All inputs are finite; a program needn't handle non-finite values.
Results may differ from a plain program's by a relative error of at most 0.015.
Values may be sent and summed in bfloat16 or wider, within the bound.
A program may use at most 128 MiB of HBM per device.

v0:
```python
import jax
import jax.numpy as jnp
from jax import lax
from jax.sharding import PartitionSpec as P

HEADS = 16
HEAD_DIM = 128
SPAN = 2


QUERY_SCALE = 1.0 / 12.0
SOFT_CAP = 50.0


def passed_along(x, axis, by):
    devices = lax.axis_size(axis)
    pairs = [(i, i + by) for i in range(devices) if 0 <= i + by < devices]
    return lax.ppermute(x, axis, pairs)


def attend_grads(query_rows, grad_rows, key_all, value_all, query_pos, key_pos, window_len):
    scores = (
        jnp.einsum("thd,khd->htk", query_rows, key_all, preferred_element_type=jnp.float32)
        * QUERY_SCALE
    )
    tanh_part = jnp.tanh(scores / SOFT_CAP)
    visible = (
        (key_pos[None, :] <= query_pos[:, None])
        & (key_pos[None, :] > query_pos[:, None] - window_len)
        & (key_pos[None, :] >= 0)
    )
    masked_exp = jnp.where(visible[None], jnp.exp(SOFT_CAP * tanh_part), 0.0)
    weights = masked_exp / jnp.sum(masked_exp, axis=2, keepdims=True)
    grad_weight = jnp.einsum(
        "thd,khd->htk", grad_rows, value_all, preferred_element_type=jnp.float32
    )
    row_dot = jnp.sum(weights * grad_weight, axis=2, keepdims=True)
    dscore = (
        weights * (grad_weight - row_dot) * (1.0 - tanh_part * tanh_part) * QUERY_SCALE
    ).astype(jnp.bfloat16)
    weight_b = weights.astype(jnp.bfloat16)
    grad_value = jnp.einsum(
        "htk,thd->khd", weight_b, grad_rows, preferred_element_type=jnp.float32
    ).astype(jnp.bfloat16)
    grad_query = jnp.einsum("htk,khd->thd", dscore, key_all, preferred_element_type=jnp.float32)
    grad_key = jnp.einsum(
        "htk,thd->khd", dscore, query_rows, preferred_element_type=jnp.float32
    ).astype(jnp.bfloat16)
    return (grad_query, grad_key, grad_value)


def on_device(saved_inputs, scale_gains, out_proj, top_grad):
    segment_count = lax.axis_size("segment")
    segment_at = lax.axis_index("segment")
    ctx_place = lax.axis_index("ctx")
    micros = saved_inputs.shape[1]
    tok_rows = saved_inputs.shape[2]
    features = saved_inputs.shape[3]
    head_count = HEADS
    head_size = HEAD_DIM
    span_count = SPAN
    lead_rows = span_count * tok_rows
    window_len = span_count * tok_rows
    query_pos = ctx_place * tok_rows + jnp.arange(tok_rows, dtype=jnp.int32)
    key_pos = ctx_place * tok_rows - lead_rows + jnp.arange(lead_rows + tok_rows, dtype=jnp.int32)
    gain_rows = scale_gains[0]
    projection = out_proj[0]
    outputs = jnp.zeros(saved_inputs.shape, jnp.bfloat16)
    received = jnp.zeros((tok_rows, features), jnp.bfloat16)
    is_top = segment_at == segment_count - 1
    last_tick = segment_count + micros - 2
    for tick_at in range(segment_count + micros - 1):
        micro_at = tick_at - (segment_count - 1 - segment_at)
        active = (micro_at >= 0) & (micro_at < micros)
        slot_at = jnp.clip(micro_at, 0, micros - 1)
        inputs = lax.dynamic_index_in_dim(saved_inputs[0], slot_at, 0, keepdims=False)
        top_piece = lax.dynamic_index_in_dim(top_grad, slot_at, 0, keepdims=False)
        grad_in = jnp.where(is_top, top_piece, received)
        input_f = inputs.astype(jnp.float32)
        query_rows = (
            (input_f * gain_rows[0]).astype(jnp.bfloat16).reshape(tok_rows, head_count, head_size)
        )
        key_rows = (
            (input_f * gain_rows[1]).astype(jnp.bfloat16).reshape(tok_rows, head_count, head_size)
        )
        value_rows = (
            (input_f * gain_rows[2]).astype(jnp.bfloat16).reshape(tok_rows, head_count, head_size)
        )
        head_grad = lax.dot_general(
            grad_in, projection, (((1,), (1,)), ((), ())), preferred_element_type=jnp.float32
        ).astype(jnp.bfloat16)
        grad_rows = head_grad.reshape(tok_rows, head_count, head_size)
        key_list = [key_rows]
        value_list = [value_rows]
        moving = (key_rows, value_rows)
        for hop_at in range(1, span_count + 1):
            moving = passed_along((moving[0], moving[1]), "ctx", 1)
            key_list.append(moving[0])
            value_list.append(moving[1])
        key_all = jnp.concatenate(key_list[::-1], axis=0)
        value_all = jnp.concatenate(value_list[::-1], axis=0)
        grad_query, grad_key, grad_value = attend_grads(
            query_rows, grad_rows, key_all, value_all, query_pos, key_pos, window_len
        )
        key_total = grad_key[lead_rows:].astype(jnp.float32)
        value_total = grad_value[lead_rows:].astype(jnp.float32)
        for hop_at in range(1, span_count + 1):
            lower = lead_rows - hop_at * tok_rows
            returned = passed_along(
                (grad_key[lower : lower + tok_rows], grad_value[lower : lower + tok_rows]),
                "ctx",
                -hop_at,
            )
            key_total = key_total + returned[0].astype(jnp.float32)
            value_total = value_total + returned[1].astype(jnp.float32)
        total = (
            grad_in.astype(jnp.float32)
            + gain_rows[0] * grad_query.reshape(tok_rows, features)
            + gain_rows[1] * key_total.reshape(tok_rows, features)
            + gain_rows[2] * value_total.reshape(tok_rows, features)
        )
        result = total.astype(jnp.bfloat16)
        current = lax.dynamic_index_in_dim(outputs[0], slot_at, 0, keepdims=False)
        chosen = jnp.where(active, result, current)
        outputs = lax.dynamic_update_slice(outputs, chosen[None, None], (0, slot_at, 0, 0))
        if tick_at < last_tick:
            received = passed_along(result, "segment", -1)
    return outputs


def solution(mesh):
    placed = (
        P("segment", None, "ctx", None),
        P("segment", None, None),
        P("segment", None, None),
        P(None, "ctx", None),
    )
    return jax.shard_map(
        on_device,
        mesh=mesh,
        in_specs=placed,
        out_specs=P("segment", None, "ctx", None),
        check_vma=False,
    )
```

profile of v0, /device:TPU:15, one launch (start us, length us, event | category | flops | bytes accessed | tf_op | source)
XLA Modules:
  0.0 687.4 jit_solution(2055057789850768837)
XLA Ops:
  32.0 7.1 %fusion.30 = bf16[128,2048]{1,0:T(8,128)(2,1)} fusion(bf16[1,2048,2048]{2,1,0:T(8,128)(2,1)} %param.6, bf16[2,128,2048]{2,1,0:T(8,128)(2,1)S(1)} %copy-done, s32[]{:T(128)S(6)} %min.16, pred[]{:T(512)S(6)} %eq.3), kind=kOutput, calls=%fused_computation.40 | convolution fusion | flops 1074266112 | bytes 9437189 | tf_op jit(solution)/shard_map/dot_general | solution.py:89
  68.1 17.9 %collective-permute-done.28 = bf16[128,16,128]{2,0,1:T(8,128)(2,1)S(1)} collective-permute-done((bf16[128,16,128]{2,0,1:T(8,128)(2,1)}, bf16[128,16,128]{2,0,1:T(8,128)(2,1)S(1)}, u32[]{:S(2)}, u32[]{:S(2)}) %collective-permute-start.28) | collective-permute-done | bytes 524320 | tf_op jit(solution)/shard_map/ppermute | solution.py:18
  122.2 20.0 %collective-permute-done.3 = bf16[128,16,128]{2,0,1:T(8,128)(2,1)S(1)} collective-permute-done((bf16[128,16,128]{2,0,1:T(8,128)(2,1)}, bf16[128,16,128]{2,0,1:T(8,128)(2,1)S(1)}, u32[]{:S(2)}, u32[]{:S(2)}) %collective-permute-start.3) | collective-permute-done | bytes 524320 | tf_op jit(solution)/shard_map/ppermute | solution.py:18
  145.8 7.6 %collective-permute-done.1 = bf16[128,16,128]{2,0,1:T(8,128)(2,1)S(1)} collective-permute-done((bf16[128,16,128]{2,0,1:T(8,128)(2,1)}, bf16[128,16,128]{2,0,1:T(8,128)(2,1)S(1)}, u32[]{:S(2)}, u32[]{:S(2)}) %collective-permute-start.1) | collective-permute-done | bytes 524320 | tf_op jit(solution)/shard_map/ppermute | solution.py:18
  155.7 9.0 %collective-permute-done.37 = bf16[128,16,128]{2,0,1:T(8,128)(2,1)S(1)} collective-permute-done((bf16[128,16,128]{2,0,1:T(8,128)(2,1)S(1)}, bf16[128,16,128]{2,0,1:T(8,128)(2,1)S(1)}, u32[]{:S(2)}, u32[]{:S(2)}) %collective-permute-start.37) | collective-permute-done | bytes 524320 | tf_op jit(solution)/shard_map/ppermute | solution.py:18
  170.6 17.4 %fusion.115 = bf16[384,16,128]{0,2,1:T(8,128)(2,1)} fusion(f32[16,128,384]{2,1,0:T(8,128)} %fusion.55, f32[16,128,384]{2,1,0:T(8,128)} %copy-done.11, f32[16,128]{1,0:T(8,128)S(1)} %bitcast.203, bf16[128,16,128]{0,2,1:T(8,128)(2,1)S(1)} %bitcast.170, f32[16,128]{1,0:T(8,128)S(1)} %get-tuple-element.9, pred[128,384]{1,0:T(8,128)(4,1)S(1)} %and_and_fusion), kind=kOutput, calls=%fused_computation.110 | convolution fusion | flops 215484800 | bytes 8454144 | tf_op jit(solution)/shard_map/htk,thd->khd/dot_general | solution.py:46
  190.3 7.8 %collective-permute-start.4 = (bf16[128,16,128]{0,2,1:T(8,128)(2,1)}, bf16[128,16,128]{0,2,1:T(8,128)(2,1)}, u32[]{:S(2)}, u32[]{:S(2)}) collective-permute-start(bf16[128,16,128]{0,2,1:T(8,128)(2,1)} %get-tuple-element.32), channel_id=1, source_target_pairs={{1,0},{2,1},{3,2},{4,3},{5,4},{6,5},{7,6},{8,7},{9,8},{10,9},{11,1... | collective-permute-start | bytes 1572872 | tf_op jit(solution)/shard_map/ppermute | solution.py:18
  211.4 17.5 %fusion.93 = f32[16,128,128]{2,1,0:T(8,128)S(1)} fusion(f32[16,128,384]{2,1,0:T(8,128)} %fusion.55, f32[16,128,384]{2,1,0:T(8,128)} %copy-done.11, bf16[128,16,128]{2,0,1:T(8,128)(2,1)} %get-tuple-element.45, bf16[128,16,128]{2,0,1:T(8,128)(2,1)} %collective-permute-done, bf16[128,16,128]{2,0,1:T(8,128)(2,1)S(1)} %collective-permute-done.1, ...), kind=kOutput, calls=%fused_computation.105 | convolution fusion | flops 218630528 | bytes 8970240 | tf_op jit(solution)/shard_map/htk,khd->thd/dot_general | solution.py:45
  258.2 11.2 %collective-permute-done.8 = bf16[128,2048]{1,0:T(8,128)(2,1)} collective-permute-done((bf16[128,2048]{1,0:T(8,128)(2,1)}, bf16[128,2048]{1,0:T(8,128)(2,1)}, u32[]{:S(2)}, u32[]{:S(2)}) %collective-permute-start.8) | collective-permute-done | bytes 524320 | tf_op jit(solution)/shard_map/ppermute | solution.py:18
  269.4 7.2 %fusion.33 = bf16[128,2048]{1,0:T(8,128)(2,1)} fusion(bf16[1,2048,2048]{2,1,0:T(8,128)(2,1)} %param.6, bf16[128,2048]{1,0:T(8,128)(2,1)} %collective-permute-done.8, bf16[2,128,2048]{2,1,0:T(8,128)(2,1)S(1)} %copy-done, s32[]{:T(128)S(6)} %min.17, pred[]{:T(512)S(6)} %eq.3), kind=kOutput, calls=%fused_computation.41 | convolution fusion | flops 1074266112 | bytes 9961477 | tf_op jit(solution)/shard_map/dot_general | solution.py:89
  281.8 17.3 %fusion.121 = bf16[384,16,128]{0,2,1:T(8,128)(2,1)} fusion(f32[16,128,384]{2,1,0:T(8,128)} %fusion.61, f32[16,128,384]{2,1,0:T(8,128)} %copy-done.10, f32[16,128]{1,0:T(8,128)S(1)} %bitcast.206, bf16[128,16,128]{0,2,1:T(8,128)(2,1)S(1)} %bitcast.167, f32[16,128]{1,0:T(8,128)S(1)} %get-tuple-element.6, pred[128,384]{1,0:T(8,128)(4,1)S(1)} %and_and_fusion), kind=kOutput, calls=%fused_computation.112 | convolution fusion | flops 215484800 | bytes 8454144 | tf_op jit(solution)/shard_map/htk,thd->khd/dot_general | solution.py:46
  316.4 18.3 %fusion.98 = f32[16,128,128]{2,1,0:T(8,128)} fusion(f32[16,128,384]{2,1,0:T(8,128)} %fusion.61, f32[16,128,384]{2,1,0:T(8,128)} %copy-done.10, bf16[128,16,128]{2,0,1:T(8,128)(2,1)} %get-tuple-element.60, bf16[128,16,128]{2,0,1:T(8,128)(2,1)} %collective-permute-done.9, bf16[128,16,128]{2,0,1:T(8,128)(2,1)S(1)} %copy-done.32, ...), kind=kOutput, calls=%fused_computation.106 | convolution fusion | flops 218630528 | bytes 8970240 | tf_op jit(solution)/shard_map/htk,khd->thd/dot_general | solution.py:45
  359.2 25.1 %collective-permute-done.17 = bf16[128,2048]{1,0:T(8,128)(2,1)S(1)} collective-permute-done((bf16[128,2048]{1,0:T(8,128)(2,1)}, bf16[128,2048]{1,0:T(8,128)(2,1)S(1)}, u32[]{:S(2)}, u32[]{:S(2)}) %collective-permute-start.17) | collective-permute-done | bytes 524320 | tf_op jit(solution)/shard_map/ppermute | solution.py:18
  385.0 7.1 %fusion.36 = bf16[128,2048]{1,0:T(8,128)(2,1)} fusion(bf16[1,2048,2048]{2,1,0:T(8,128)(2,1)} %param.6, bf16[128,2048]{1,0:T(8,128)(2,1)S(1)} %collective-permute-done.17, bf16[2,128,2048]{2,1,0:T(8,128)(2,1)S(1)} %copy-done, s32[]{:T(128)S(6)} %min.18, pred[]{:T(512)S(6)} %eq.3), kind=kOutput, calls=%fused_computation.42 | convolution fusion | flops 1074266112 | bytes 9961477 | tf_op jit(solution)/shard_map/dot_general | solution.py:89
  397.4 17.4 %fusion.127 = bf16[384,16,128]{0,2,1:T(8,128)(2,1)} fusion(f32[16,128,384]{2,1,0:T(8,128)} %fusion.67, f32[16,128,384]{2,1,0:T(8,128)} %copy-done.9, f32[16,128]{1,0:T(8,128)S(1)} %bitcast.208, bf16[128,16,128]{0,2,1:T(8,128)(2,1)S(1)} %bitcast.164, f32[16,128]{1,0:T(8,128)S(1)} %get-tuple-element.7, pred[128,384]{1,0:T(8,128)(4,1)S(1)} %and_and_fusion), kind=kOutput, calls=%fused_computation.114 | convolution fusion | flops 215484800 | bytes 8454144 | tf_op jit(solution)/shard_map/htk,thd->khd/dot_general | solution.py:46
  435.6 18.3 %fusion.103 = f32[16,128,128]{2,1,0:T(8,128)} fusion(f32[16,128,384]{2,1,0:T(8,128)} %fusion.67, f32[16,128,384]{2,1,0:T(8,128)} %copy-done.9, bf16[128,16,128]{2,0,1:T(8,128)(2,1)} %get-tuple-element.58, bf16[128,16,128]{2,0,1:T(8,128)(2,1)} %collective-permute-done.18, bf16[128,16,128]{2,0,1:T(8,128)(2,1)S(1)} %copy-done.30, ...), kind=kOutput, calls=%fused_computation.107 | convolution fusion | flops 218630528 | bytes 8970240 | tf_op jit(solution)/shard_map/htk,khd->thd/dot_general | solution.py:45
  477.1 26.5 %collective-permute-done.26 = bf16[128,2048]{1,0:T(8,128)(2,1)S(1)} collective-permute-done((bf16[128,2048]{1,0:T(8,128)(2,1)}, bf16[128,2048]{1,0:T(8,128)(2,1)S(1)}, u32[]{:S(2)}, u32[]{:S(2)}) %collective-permute-start.26) | collective-permute-done | bytes 524320 | tf_op jit(solution)/shard_map/ppermute | solution.py:18
  504.4 7.1 %fusion.39 = bf16[128,2048]{1,0:T(8,128)(2,1)} fusion(bf16[1,2048,2048]{2,1,0:T(8,128)(2,1)} %param.6, bf16[128,2048]{1,0:T(8,128)(2,1)S(1)} %collective-permute-done.26, bf16[2,128,2048]{2,1,0:T(8,128)(2,1)S(1)} %copy-done, s32[]{:T(128)S(6)} %min.19, pred[]{:T(512)S(6)} %eq.3), kind=kOutput, calls=%fused_computation.43 | convolution fusion | flops 1074266112 | bytes 9961477 | tf_op jit(solution)/shard_map/dot_general | solution.py:89
  516.7 17.5 %fusion.133 = bf16[384,16,128]{0,2,1:T(8,128)(2,1)} fusion(f32[16,128,384]{2,1,0:T(8,128)} %fusion.73, f32[16,128,384]{2,1,0:T(8,128)} %copy-done.8, f32[16,128]{1,0:T(8,128)S(1)} %bitcast.210, bf16[128,16,128]{0,2,1:T(8,128)(2,1)S(1)} %bitcast.161, f32[16,128]{1,0:T(8,128)S(1)} %get-tuple-element.8, pred[128,384]{1,0:T(8,128)(4,1)S(1)} %and_and_fusion), kind=kOutput, calls=%fused_computation.116 | convolution fusion | flops 215484800 | bytes 8454144 | tf_op jit(solution)/shard_map/htk,thd->khd/dot_general | solution.py:46
  555.2 18.5 %fusion.108 = f32[16,128,128]{2,1,0:T(8,128)} fusion(f32[16,128,384]{2,1,0:T(8,128)} %fusion.73, f32[16,128,384]{2,1,0:T(8,128)} %copy-done.8, bf16[128,16,128]{2,0,1:T(8,128)(2,1)} %get-tuple-element.56, bf16[128,16,128]{2,0,1:T(8,128)(2,1)} %collective-permute-done.27, bf16[128,16,128]{2,0,1:T(8,128)(2,1)S(1)} %copy-done.28, ...), kind=kOutput, calls=%fused_computation.108 | convolution fusion | flops 218630528 | bytes 8970240 | tf_op jit(solution)/shard_map/htk,khd->thd/dot_general | solution.py:45
  594.7 17.4 %collective-permute-done.35 = bf16[128,2048]{1,0:T(8,128)(2,1)S(1)} collective-permute-done((bf16[128,2048]{1,0:T(8,128)(2,1)}, bf16[128,2048]{1,0:T(8,128)(2,1)S(1)}, u32[]{:S(2)}, u32[]{:S(2)}) %collective-permute-start.35) | collective-permute-done | bytes 524320 | tf_op jit(solution)/shard_map/ppermute | solution.py:18
  612.1 7.3 %fusion.42 = bf16[128,2048]{1,0:T(8,128)(2,1)} fusion(bf16[1,2048,2048]{2,1,0:T(8,128)(2,1)} %param.6, bf16[128,2048]{1,0:T(8,128)(2,1)S(1)} %collective-permute-done.35, bf16[2,128,2048]{2,1,0:T(8,128)(2,1)S(1)} %copy-done, s32[]{:T(128)S(6)} %min.20, pred[]{:T(512)S(6)} %eq.3), kind=kOutput, calls=%fused_computation.44 | convolution fusion | flops 1074266112 | bytes 9961477 | tf_op jit(solution)/shard_map/dot_general | solution.py:89
  625.5 17.4 %fusion.139 = bf16[384,16,128]{0,2,1:T(8,128)(2,1)} fusion(f32[16,128,384]{2,1,0:T(8,128)} %fusion.79, f32[16,128,384]{2,1,0:T(8,128)} %get-tuple-element.62, f32[16,128]{1,0:T(8,128)S(1)} %bitcast.212, bf16[128,16,128]{0,2,1:T(8,128)(2,1)S(1)} %bitcast.183, f32[16,128]{1,0:T(8,128)S(1)} %get-tuple-element.5, pred[128,384]{1,0:T(8,128)(4,1)S(1)} %and_and_fusion), kind=kOutput, calls=%fused_computation.118 | convolution fusion | flops 215484800 | bytes 8454144 | tf_op jit(solution)/shard_map/htk,thd->khd/dot_general | solution.py:46
  660.3 17.6 %fusion.113 = f32[16,128,128]{2,1,0:T(8,128)S(1)} fusion(f32[16,128,384]{2,1,0:T(8,128)} %fusion.79, f32[16,128,384]{2,1,0:T(8,128)} %get-tuple-element.62, bf16[128,16,128]{2,0,1:T(8,128)(2,1)S(1)} %copy-done.26, bf16[128,16,128]{2,0,1:T(8,128)(2,1)S(1)} %copy-done.36, bf16[128,16,128]{2,0,1:T(8,128)(2,1)} %copy-done.37, ...), kind=kOutput, calls=%fused_computation.109 | convolution fusion | flops 218630528 | bytes 8970240 | tf_op jit(solution)/shard_map/htk,khd->thd/dot_general | solution.py:45
  (241 shorter events, 330.5 us)
Async XLA Ops:
  15.3 77.4 %collective-permute-start.2 = (bf16[128,16,128]{2,0,1:T(8,128)(2,1)}, bf16[128,16,128]{2,0,1:T(8,128)(2,1)}, u32[]{:S(2)}, u32[]{:S(2)}) collective-permute-start(bf16[128,16,128]{2,0,1:T(8,128)(2,1)} %get-tuple-element.44), channel_id=1, source_target_pairs={{0,1},{1,2},{2,3},{3,4},{4,5},{5,6},{6,7},{7,8},{8,9},{9,10},{10,1... | collective-permute-start | bytes 1572872 | tf_op jit(solution)/shard_map/ppermute | solution.py:18
  25.4 38.3 %collective-permute-start.9 = (bf16[128,16,128]{2,0,1:T(8,128)(2,1)}, bf16[128,16,128]{2,0,1:T(8,128)(2,1)}, u32[]{:S(2)}, u32[]{:S(2)}) collective-permute-start(bf16[128,16,128]{2,0,1:T(8,128)(2,1)} %get-tuple-element.60), channel_id=1, source_target_pairs={{0,1},{1,2},{2,3},{3,4},{4,5},{5,6},{6,7},{7,8},{8,9},{9,10},{10,1... | collective-permute-start | bytes 1572872 | tf_op jit(solution)/shard_map/ppermute | solution.py:18
  28.6 66.4 %collective-permute-start = (bf16[128,16,128]{2,0,1:T(8,128)(2,1)}, bf16[128,16,128]{2,0,1:T(8,128)(2,1)}, u32[]{:S(2)}, u32[]{:S(2)}) collective-permute-start(bf16[128,16,128]{2,0,1:T(8,128)(2,1)} %get-tuple-element.45), channel_id=1, source_target_pairs={{0,1},{1,2},{2,3},{3,4},{4,5},{5,6},{6,7},{7,8},{8,9},{9,10},{10,1... | collective-permute-start | bytes 1572872 | tf_op jit(solution)/shard_map/ppermute | solution.py:18
  41.2 44.8 %collective-permute-start.28 = (bf16[128,16,128]{2,0,1:T(8,128)(2,1)}, bf16[128,16,128]{2,0,1:T(8,128)(2,1)S(1)}, u32[]{:S(2)}, u32[]{:S(2)}) collective-permute-start(bf16[128,16,128]{2,0,1:T(8,128)(2,1)} %collective-permute-done.27), channel_id=1, source_target_pairs={{0,1},{1,2},{2,3},{3,4},{4,5},{5,6},{6,7},{7,8},{8,9},{9,10},{10,1... | collective-permute-start | bytes 1572872 | tf_op jit(solution)/shard_map/ppermute | solution.py:18
  52.4 46.9 %collective-permute-start.36 = (bf16[128,16,128]{2,0,1:T(8,128)(2,1)}, bf16[128,16,128]{2,0,1:T(8,128)(2,1)S(1)}, u32[]{:S(2)}, u32[]{:S(2)}) collective-permute-start(bf16[128,16,128]{2,0,1:T(8,128)(2,1)} %get-tuple-element.54), channel_id=1, source_target_pairs={{0,1},{1,2},{2,3},{3,4},{4,5},{5,6},{6,7},{7,8},{8,9},{9,10},{10,1... | collective-permute-start | bytes 1572872 | tf_op jit(solution)/shard_map/ppermute | solution.py:18
  63.6 44.8 %collective-permute-start.19 = (bf16[128,16,128]{2,0,1:T(8,128)(2,1)}, bf16[128,16,128]{2,0,1:T(8,128)(2,1)S(1)}, u32[]{:S(2)}, u32[]{:S(2)}) collective-permute-start(bf16[128,16,128]{2,0,1:T(8,128)(2,1)} %collective-permute-done.18), channel_id=1, source_target_pairs={{0,1},{1,2},{2,3},{3,4},{4,5},{5,6},{6,7},{7,8},{8,9},{9,10},{10,1... | collective-permute-start | bytes 1572872 | tf_op jit(solution)/shard_map/ppermute | solution.py:18
  92.7 138.9 %collective-permute-start.11 = (bf16[128,16,128]{2,0,1:T(8,128)(2,1)}, bf16[128,16,128]{2,0,1:T(8,128)(2,1)}, u32[]{:S(2)}, u32[]{:S(2)}) collective-permute-start(bf16[128,16,128]{2,0,1:T(8,128)(2,1)} %get-tuple-element.61), channel_id=1, source_target_pairs={{0,1},{1,2},{2,3},{3,4},{4,5},{5,6},{6,7},{7,8},{8,9},{9,10},{10,1... | collective-permute-start | bytes 1572872 | tf_op jit(solution)/shard_map/ppermute | solution.py:18
  95.0 47.2 %collective-permute-start.3 = (bf16[128,16,128]{2,0,1:T(8,128)(2,1)}, bf16[128,16,128]{2,0,1:T(8,128)(2,1)S(1)}, u32[]{:S(2)}, u32[]{:S(2)}) collective-permute-start(bf16[128,16,128]{2,0,1:T(8,128)(2,1)} %collective-permute-done.2), channel_id=1, source_target_pairs={{0,1},{1,2},{2,3},{3,4},{4,5},{5,6},{6,7},{7,8},{8,9},{9,10},{10,1... | collective-permute-start | bytes 1572872 | tf_op jit(solution)/shard_map/ppermute | solution.py:18
  99.3 54.1 %collective-permute-start.1 = (bf16[128,16,128]{2,0,1:T(8,128)(2,1)}, bf16[128,16,128]{2,0,1:T(8,128)(2,1)S(1)}, u32[]{:S(2)}, u32[]{:S(2)}) collective-permute-start(bf16[128,16,128]{2,0,1:T(8,128)(2,1)} %collective-permute-done), channel_id=1, source_target_pairs={{0,1},{1,2},{2,3},{3,4},{4,5},{5,6},{6,7},{7,8},{8,9},{9,10},{10,1... | collective-permute-start | bytes 1572872 | tf_op jit(solution)/shard_map/ppermute | solution.py:18
  108.5 56.2 %collective-permute-start.37 = (bf16[128,16,128]{2,0,1:T(8,128)(2,1)S(1)}, bf16[128,16,128]{2,0,1:T(8,128)(2,1)S(1)}, u32[]{:S(2)}, u32[]{:S(2)}) collective-permute-start(bf16[128,16,128]{2,0,1:T(8,128)(2,1)S(1)} %collective-permute-done.36), channel_id=1, source_target_pairs={{0,1},{1,2},{2,3},{3,4},{4,5},{5,6},{6,7},{7,8},{8,9},{9,10},{10,1... | collective-permute-start | bytes 1572872 | tf_op jit(solution)/shard_map/ppermute | solution.py:18
  190.3 44.7 %collective-permute-start.4 = (bf16[128,16,128]{0,2,1:T(8,128)(2,1)}, bf16[128,16,128]{0,2,1:T(8,128)(2,1)}, u32[]{:S(2)}, u32[]{:S(2)}) collective-permute-start(bf16[128,16,128]{0,2,1:T(8,128)(2,1)} %get-tuple-element.32), channel_id=1, source_target_pairs={{1,0},{2,1},{3,2},{4,3},{5,4},{6,5},{7,6},{8,7},{9,8},{10,9},{11,1... | collective-permute-start | bytes 1572872 | tf_op jit(solution)/shard_map/ppermute | solution.py:18
  198.1 39.2 %collective-permute-start.5 = (bf16[128,16,128]{0,2,1:T(8,128)(2,1)}, bf16[128,16,128]{0,2,1:T(8,128)(2,1)}, u32[]{:S(2)}, u32[]{:S(2)}) collective-permute-start(bf16[128,16,128]{0,2,1:T(8,128)(2,1)} %get-tuple-element.33), channel_id=1, source_target_pairs={{2,0},{3,1},{4,2},{5,3},{6,4},{7,5},{8,6},{9,7},{10,8},{11,9},{12,... | collective-permute-start | bytes 1572872 | tf_op jit(solution)/shard_map/ppermute | solution.py:18
  231.5 123.5 %collective-permute-start.20 = (bf16[128,16,128]{2,0,1:T(8,128)(2,1)}, bf16[128,16,128]{2,0,1:T(8,128)(2,1)}, u32[]{:S(2)}, u32[]{:S(2)}) collective-permute-start(bf16[128,16,128]{2,0,1:T(8,128)(2,1)} %get-tuple-element.59), channel_id=1, source_target_pairs={{0,1},{1,2},{2,3},{3,4},{4,5},{5,6},{6,7},{7,8},{8,9},{9,10},{10,1... | collective-permute-start | bytes 1572872 | tf_op jit(solution)/shard_map/ppermute | solution.py:18
  235.0 43.0 %collective-permute-start.12 = (bf16[128,16,128]{2,0,1:T(8,128)(2,1)}, bf16[128,16,128]{2,0,1:T(8,128)(2,1)}, u32[]{:S(2)}, u32[]{:S(2)}) collective-permute-start(bf16[128,16,128]{2,0,1:T(8,128)(2,1)} %collective-permute-done.11), channel_id=1, source_target_pairs={{0,1},{1,2},{2,3},{3,4},{4,5},{5,6},{6,7},{7,8},{8,9},{9,10},{10,1... | collective-permute-start | bytes 1572872 | tf_op jit(solution)/shard_map/ppermute | solution.py:18
  301.5 34.8 %collective-permute-start.13 = (bf16[128,16,128]{0,2,1:T(8,128)(2,1)}, bf16[128,16,128]{0,2,1:T(8,128)(2,1)}, u32[]{:S(2)}, u32[]{:S(2)}) collective-permute-start(bf16[128,16,128]{0,2,1:T(8,128)(2,1)} %get-tuple-element.28), channel_id=1, source_target_pairs={{1,0},{2,1},{3,2},{4,3},{5,4},{6,5},{7,6},{8,7},{9,8},{10,9},{11,1... | collective-permute-start | bytes 1572872 | tf_op jit(solution)/shard_map/ppermute | solution.py:18
  349.6 34.7 %collective-permute-start.17 = (bf16[128,2048]{1,0:T(8,128)(2,1)}, bf16[128,2048]{1,0:T(8,128)(2,1)S(1)}, u32[]{:S(2)}, u32[]{:S(2)}) collective-permute-start(bf16[128,2048]{1,0:T(8,128)(2,1)} %get-tuple-element.15), channel_id=1, source_target_pairs={{64,0},{128,64},{192,128},{65,1},{129,65},{193,129},{66,2},{130,66... | collective-permute-start | bytes 1572872 | tf_op jit(solution)/shard_map/ppermute | solution.py:18
  351.5 121.3 %collective-permute-start.29 = (bf16[128,16,128]{2,0,1:T(8,128)(2,1)}, bf16[128,16,128]{2,0,1:T(8,128)(2,1)}, u32[]{:S(2)}, u32[]{:S(2)}) collective-permute-start(bf16[128,16,128]{2,0,1:T(8,128)(2,1)} %get-tuple-element.57), channel_id=1, source_target_pairs={{0,1},{1,2},{2,3},{3,4},{4,5},{5,6},{6,7},{7,8},{8,9},{9,10},{10,1... | collective-permute-start | bytes 1572872 | tf_op jit(solution)/shard_map/ppermute | solution.py:18
  355.0 38.4 %collective-permute-start.21 = (bf16[128,16,128]{2,0,1:T(8,128)(2,1)}, bf16[128,16,128]{2,0,1:T(8,128)(2,1)}, u32[]{:S(2)}, u32[]{:S(2)}) collective-permute-start(bf16[128,16,128]{2,0,1:T(8,128)(2,1)} %collective-permute-done.20), channel_id=1, source_target_pairs={{0,1},{1,2},{2,3},{3,4},{4,5},{5,6},{6,7},{7,8},{8,9},{9,10},{10,1... | collective-permute-start | bytes 1572872 | tf_op jit(solution)/shard_map/ppermute | solution.py:18
  417.2 38.4 %collective-permute-start.22 = (bf16[128,16,128]{0,2,1:T(8,128)(2,1)}, bf16[128,16,128]{0,2,1:T(8,128)(2,1)}, u32[]{:S(2)}, u32[]{:S(2)}) collective-permute-start(bf16[128,16,128]{0,2,1:T(8,128)(2,1)} %get-tuple-element.24), channel_id=1, source_target_pairs={{1,0},{2,1},{3,2},{4,3},{5,4},{6,5},{7,6},{8,7},{9,8},{10,9},{11,1... | collective-permute-start | bytes 1572872 | tf_op jit(solution)/shard_map/ppermute | solution.py:18
  419.1 36.5 %collective-permute-start.23 = (bf16[128,16,128]{0,2,1:T(8,128)(2,1)}, bf16[128,16,128]{0,2,1:T(8,128)(2,1)}, u32[]{:S(2)}, u32[]{:S(2)}) collective-permute-start(bf16[128,16,128]{0,2,1:T(8,128)(2,1)} %get-tuple-element.25), channel_id=1, source_target_pairs={{2,0},{3,1},{4,2},{5,3},{6,4},{7,5},{8,6},{9,7},{10,8},{11,9},{12,... | collective-permute-start | bytes 1572872 | tf_op jit(solution)/shard_map/ppermute | solution.py:18
  470.8 119.7 %collective-permute-start.38 = (bf16[128,16,128]{2,0,1:T(8,128)(2,1)}, bf16[128,16,128]{2,0,1:T(8,128)(2,1)}, u32[]{:S(2)}, u32[]{:S(2)}) collective-permute-start(bf16[128,16,128]{2,0,1:T(8,128)(2,1)} %get-tuple-element.55), channel_id=1, source_target_pairs={{0,1},{1,2},{2,3},{3,4},{4,5},{5,6},{6,7},{7,8},{8,9},{9,10},{10,1... | collective-permute-start | bytes 1572872 | tf_op jit(solution)/shard_map/ppermute | solution.py:18
  472.8 40.0 %collective-permute-start.30 = (bf16[128,16,128]{2,0,1:T(8,128)(2,1)}, bf16[128,16,128]{2,0,1:T(8,128)(2,1)}, u32[]{:S(2)}, u32[]{:S(2)}) collective-permute-start(bf16[128,16,128]{2,0,1:T(8,128)(2,1)} %collective-permute-done.29), channel_id=1, source_target_pairs={{0,1},{1,2},{2,3},{3,4},{4,5},{5,6},{6,7},{7,8},{8,9},{9,10},{10,1... | collective-permute-start | bytes 1572872 | tf_op jit(solution)/shard_map/ppermute | solution.py:18
  536.5 38.8 %collective-permute-start.31 = (bf16[128,16,128]{0,2,1:T(8,128)(2,1)}, bf16[128,16,128]{0,2,1:T(8,128)(2,1)}, u32[]{:S(2)}, u32[]{:S(2)}) collective-permute-start(bf16[128,16,128]{0,2,1:T(8,128)(2,1)} %get-tuple-element.20), channel_id=1, source_target_pairs={{1,0},{2,1},{3,2},{4,3},{5,4},{6,5},{7,6},{8,7},{9,8},{10,9},{11,1... | collective-permute-start | bytes 1572872 | tf_op jit(solution)/shard_map/ppermute | solution.py:18
  538.5 36.9 %collective-permute-start.32 = (bf16[128,16,128]{0,2,1:T(8,128)(2,1)}, bf16[128,16,128]{0,2,1:T(8,128)(2,1)}, u32[]{:S(2)}, u32[]{:S(2)}) collective-permute-start(bf16[128,16,128]{0,2,1:T(8,128)(2,1)} %get-tuple-element.21), channel_id=1, source_target_pairs={{2,0},{3,1},{4,2},{5,3},{6,4},{7,5},{8,6},{9,7},{10,8},{11,9},{12,... | collective-permute-start | bytes 1572872 | tf_op jit(solution)/shard_map/ppermute | solution.py:18
  (58 other events, 1476.9 us)
where the time goes:
time: 696 us; the launch traced here: 687 us
  matrix products  264 us (38%)
  waiting for transfers between devices  160 us (23%)
  starting transfers between devices  140 us (20%)
  local copies, waits for them, and re-layouts  77.3 us (11%)
  other arithmetic  45 us (6%)
    ppermute x44, waiting for transfers between devices, passed_along(): return lax.ppermute(x, axis, pairs)  160 us
    ppermute x44, starting transfers between devices, passed_along(): return lax.ppermute(x, axis, pairs)  140 us
    dot_general x5, matrix products, attend_grads(): jnp.einsum('htk,khd->thd', dscore, key_all, preferred_element_type=jnp.fl...  90.4 us
    dot_general x5, matrix products, attend_grads(): jnp.einsum('htk,thd->khd', dscore, query_rows, preferred_element_type=jnp...  87.1 us
    dot_general x5, matrix products, on_device(): lax.dot_general(grad_in, projection, (((1,), (1,)), ((), ())), preferred_...  35.7 us
    dot_general x5, matrix products, attend_grads(): jnp.einsum('thd,khd->htk', grad_rows, value_all, preferred_element_type=j...  19.2 us
    dot_general x5, matrix products, attend_grads(): jnp.einsum('htk,thd->khd', weight_b, grad_rows, preferred_element_type=jn...  16.2 us
    dot_general x5, matrix products, attend_grads(): jnp.einsum('thd,khd->htk', query_rows, key_all, preferred_element_type=jn...  15.1 us
  transfers between devices with their start and end apart: 44, of which 12 were waited for; matrix products, arithmetic and copies ran while one was open for 49% of the time, Pallas kernels for 0%

commit v1 on v0

v1 whole, which is shorter than its diff:
```python
import functools

import jax
import jax.numpy as jnp
from jax import lax
from jax.experimental import pallas as pl
from jax.experimental.pallas import tpu as pltpu
from jax.sharding import PartitionSpec as P

HEAD_DIM = 128
X_HEADS = 2
G_HEADS = 2
QUERY_SCALE = 1.0 / 12.0
SOFT_CAP = 50.0
MESH = pl.DeviceIdType.MESH
F32 = jnp.float32
BF16 = jnp.bfloat16
NT = (((1,), (1,)), ((), ()))


def cols(at, width):
    return pl.ds(pl.multiple_of(at * width, width), width)


def dot_nt(a, b):
    return lax.dot_general(a, b, NT, preferred_element_type=F32)


def dot_nn(a, b):
    return jnp.dot(a, b, preferred_element_type=F32)


def cascade_kernel(
    pair_count,
    x_hbm,
    gain_hbm,
    w_hbm,
    top_hbm,
    out_hbm,
    x_own,
    x_halo,
    gains,
    w_buf,
    g_buf,
    v_all,
    kg_all,
    qg_all,
    o_all,
    slopes,
    weight_t,
    hg_buf,
    acc,
    con_send,
    con_recv,
    gain_send_sem,
    gain_sem,
    w_send_sem,
    w_sem,
    top_sem,
    x_send_sem,
    x_sem,
    halo_send_sem,
    halo_sem,
    con_send_sem,
    con_sem,
    swap_send_sem,
    swap_sem,
    cross_send_sem,
    cross_sem,
    out_send_sem,
    out_sem,
):
    rows = x_hbm.shape[1]
    features = x_hbm.shape[2]
    half_width = features // 2
    heads = half_width // HEAD_DIM
    x_width = X_HEADS * HEAD_DIM
    g_width = G_HEADS * HEAD_DIM
    x_chunks = half_width // x_width
    g_chunks = half_width // g_width

    seg = lax.axis_index("segment")
    ctx = lax.axis_index("ctx")
    half = seg // 2
    core = seg % 2
    pair = ctx // 2
    side = ctx % 2
    upper = half == 1
    lower = half == 0
    mine = jnp.where(upper, side, 1 - side)
    held = 1 - core

    def place(half_at, core_at, pair_at, side_at):
        return (2 * half_at + core_at, 2 * pair_at + side_at)

    partner = place(half, 1 - core, pair, side)
    facing = place(1 - half, core, pair, 1 - side)
    later = place(half, core, lax.rem(pair + 1, pair_count), side)
    earlier = place(half, core, lax.rem(pair + pair_count - 1, pair_count), side)
    beside = place(half, core, pair, 1 - side)
    across = place(half, 1 - core, pair, 1 - side)

    def remote(src, dst, send_sem, recv_sem, device):
        return pltpu.make_async_remote_copy(
            src_ref=src,
            dst_ref=dst,
            send_sem=send_sem,
            recv_sem=recv_sem,
            device_id=device,
            device_id_type=MESH,
        )

    def gain_local():
        return pltpu.make_async_copy(
            gain_hbm.at[:, :, cols(core, half_width)], gains.at[held], gain_sem.at[held]
        )

    def gain_remote():
        return remote(
            gain_hbm.at[:, :, cols(1 - core, half_width)],
            gains.at[held],
            gain_send_sem,
            gain_sem.at[held],
            partner,
        )

    def gain_arrival(stage):
        return pltpu.make_async_copy(
            gain_hbm.at[:, :, cols(core, half_width)], gains.at[stage], gain_sem.at[stage]
        )

    def w_local():
        return pltpu.make_async_copy(
            w_hbm.at[cols(core, half_width), :], w_buf.at[held], w_sem.at[held]
        )

    def w_remote():
        return remote(
            w_hbm.at[cols(1 - core, half_width), :],
            w_buf.at[held],
            w_send_sem,
            w_sem.at[held],
            partner,
        )

    def w_arrival(stage):
        return pltpu.make_async_copy(
            w_hbm.at[cols(core, half_width), :], w_buf.at[stage], w_sem.at[stage]
        )

    def top_local():
        return pltpu.make_async_copy(
            top_hbm.at[mine], g_buf.at[0, cols(side, rows), :], top_sem
        )

    def x_local(i):
        return pltpu.make_async_copy(
            x_hbm.at[mine, :, cols(core * x_chunks + i, x_width)],
            x_own.at[held, cols(side, rows), cols(i, x_width)],
            x_sem.at[held, side, i],
        )

    def x_remote(i, way):
        micro = mine if way == 0 else 1 - mine
        core_at = core if way == 1 else 1 - core
        return remote(
            x_hbm.at[micro, :, cols(core_at * x_chunks + i, x_width)],
            x_own.at[held, cols(side, rows), cols(i, x_width)],
            x_send_sem.at[way, i],
            x_sem.at[held, side, i],
            (partner, beside, across)[way],
        )

    def x_arrival(stage, block, i):
        return pltpu.make_async_copy(
            x_hbm.at[mine, :, cols(core * x_chunks + i, x_width)],
            x_own.at[stage, cols(block, rows), cols(i, x_width)],
            x_sem.at[stage, block, i],
        )

    def halo_copy(stage, i):
        return remote(
            x_own.at[stage, :, cols(i, x_width)],
            x_halo.at[stage, :, cols(i, x_width)],
            halo_send_sem.at[stage, i],
            halo_sem.at[stage, i],
            later,
        )

    def con_copy(stage, h):
        return remote(
            con_send.at[stage, :, cols(h, HEAD_DIM)],
            con_recv.at[stage, :, cols(h, HEAD_DIM)],
            con_send_sem.at[stage, h],
            con_sem.at[stage, h],
            earlier,
        )

    def swap_copy(stage, f, core_at):
        ref = g_buf.at[stage, :, cols(core_at * g_chunks + f, g_width)]
        return remote(ref, ref, swap_send_sem.at[stage, f], swap_sem.at[stage, f], partner)

    def top_swap_copy(f, core_at):
        ref = g_buf.at[0, cols(1 - side, rows), cols(core_at * g_chunks + f, g_width)]
        return remote(ref, ref, swap_send_sem.at[0, f], swap_sem.at[0, f], partner)

    def down_copy(f):
        at = cols(core * g_chunks + f, g_width)
        return remote(
            g_buf.at[2, :, at], g_buf.at[0, :, at], cross_send_sem.at[f], cross_sem.at[f], facing
        )

    def top_copy(f, block):
        at = cols(core * g_chunks + f, g_width)
        return remote(
            top_hbm.at[mine, :, at],
            g_buf.at[0, cols(block, rows), at],
            cross_send_sem.at[f],
            cross_sem.at[f],
            facing,
        )

    def out_refs(stage, f, block):
        at = cols(core * g_chunks + f, g_width)
        return g_buf.at[stage + 1, cols(block, rows), at], out_hbm.at[mine, :, at]

    def out_local(stage, f):
        src, dst = out_refs(stage, f, side)
        return pltpu.make_async_copy(src, dst, out_sem.at[mine, core, f])

    def out_partner(stage, f):
        src, dst = out_refs(stage, f, side)
        return remote(
            src, dst, out_send_sem.at[stage, 0, f], out_sem.at[mine, core, f], partner
        )

    def out_beside(stage, f):
        src, dst = out_refs(stage, f, 1 - side)
        return remote(
            src,
            dst,
            out_send_sem.at[stage, 1, f],
            out_sem.at[mine, core, f],
            place(half, 1 - stage, pair, 1 - side),
        )

    def out_arrival(micro, core_at, f):
        at = cols(core_at * g_chunks + f, g_width)
        return pltpu.make_async_copy(
            g_buf.at[1, cols(0, rows), at], out_hbm.at[micro, :, at], out_sem.at[micro, core_at, f]
        )

    gain_local().start()
    for i in range(x_chunks):
        x_local(i).start()
    w_local().start()

    @pl.when(upper)
    def _():
        top_local().start()

    barrier = pltpu.get_barrier_semaphore()
    peers = (partner, facing, later, earlier, beside, across)
    for peer in peers:
        pl.semaphore_signal(barrier, inc=1, device_id=peer, device_id_type=MESH)
    pl.semaphore_wait(barrier, len(peers))

    def deliver():
        for i in range(x_chunks):
            for way in range(3):
                x_remote(i, way).start()

    @pl.when(core == 1)
    def _():
        deliver()

    gain_remote().start()

    @pl.when(lower)
    def _():
        for f in range(g_chunks):
            top_copy(f, side).start()

    w_remote().start()

    def forward(stage):
        for i in range(x_chunks):
            for block in range(2):
                x_arrival(stage, block, i).wait()
            halo_copy(stage, i).start()

    forward(0)

    @pl.when(core == 0)
    def _():
        deliver()

    for stage in range(2):
        gain_arrival(stage).wait()

    row_at = lax.broadcasted_iota(jnp.int32, (rows, rows), 0)
    col_at = lax.broadcasted_iota(jnp.int32, (rows, rows), 1)
    own = col_at <= row_at
    own_t = row_at <= col_at
    seen = (pair >= 1).astype(F32)

    def prepare_head(stage, h):
        at = cols(h, HEAD_DIM)
        gq, gk, gv = (gains[stage, n, :, at] for n in range(3))
        x = jnp.concatenate([x_halo[stage, :, at], x_own[stage, :, at]], axis=0).astype(F32)
        q = (x[2 * rows :] * gq).astype(BF16)
        k = (x * gk).astype(BF16)
        v = (x * gv).astype(BF16)
        v_all[stage, h] = v
        kg_all[stage, h] = (k.astype(F32) * gq).astype(BF16)
        qg_all[stage, h] = (q.astype(F32) * gk).astype(BF16)
        for block in range(2):
            low = block * rows
            span = slice(low, low + 3 * rows)
            s = dot_nt(q[low : low + rows], k[span]) * (QUERY_SCALE / SOFT_CAP)
            t_one = jnp.tanh(s[:, rows : 2 * rows])
            t_mix = jnp.tanh(jnp.where(own, s[:, 2 * rows :], s[:, :rows]))
            e_one = jnp.exp(SOFT_CAP * t_one)
            if block == 0:
                e_one = e_one * seen
            e_mix = jnp.exp(SOFT_CAP * t_mix)
            e_mix = jnp.where(own, e_mix, e_mix * seen)
            scale = 1.0 / jnp.sum(e_one + e_mix, axis=1, keepdims=True)
            w_one = e_one * scale
            w_mix = e_mix * scale
            slopes[stage, h, block, 0] = w_one * (1.0 - t_one * t_one) * QUERY_SCALE
            slopes[stage, h, block, 1] = w_mix * (1.0 - t_mix * t_mix) * QUERY_SCALE
            w_cat = jnp.concatenate(
                [jnp.where(own, 0.0, w_mix), w_one, jnp.where(own, w_mix, 0.0)], axis=1
            ).astype(BF16)
            o_all[stage, low : low + rows, at] = dot_nn(w_cat, v[span])
            wt_mix = w_mix.T
            weight_t[stage, h, block] = jnp.concatenate(
                [jnp.where(own_t, 0.0, wt_mix), w_one.T, jnp.where(own_t, wt_mix, 0.0)], axis=0
            ).astype(BF16)

    def attend_head(stage, h):
        at = cols(h, HEAD_DIM)
        gv = gains[stage, 2, :, at]
        both = []
        d_query = []
        for block in range(2):
            low = block * rows
            hg = hg_buf[low : low + rows, at]
            hg_f = hg.astype(F32)
            gw = dot_nt(hg, v_all[stage, h, low : low + 3 * rows])
            row_dot = jnp.sum(hg_f * o_all[stage, low : low + rows, at], axis=1, keepdims=True)
            d_one = slopes[stage, h, block, 0] * (gw[:, rows : 2 * rows] - row_dot)
            d_mix = slopes[stage, h, block, 1] * (
                jnp.where(own, gw[:, 2 * rows :], gw[:, :rows]) - row_dot
            )
            d_cat = jnp.concatenate(
                [jnp.where(own, 0.0, d_mix), d_one, jnp.where(own, d_mix, 0.0)], axis=1
            ).astype(BF16)
            dt_mix = d_mix.T
            d_t = jnp.concatenate(
                [jnp.where(own_t, 0.0, dt_mix), d_one.T, jnp.where(own_t, dt_mix, 0.0)], axis=0
            ).astype(BF16)
            left = jnp.concatenate([d_t, weight_t[stage, h, block]], axis=1)
            right = jnp.concatenate(
                [qg_all[stage, h, low : low + rows], (hg_f * gv).astype(BF16)], axis=0
            )
            both.append(dot_nn(left, right))
            d_query.append(dot_nn(d_cat, kg_all[stage, h, low : low + 3 * rows]))
        con_send[stage, :rows, at] = both[0][:rows].astype(BF16)
        con_send[stage, rows:, at] = (both[0][rows : 2 * rows] + both[1][:rows]).astype(BF16)
        g_at = cols(core * heads + h, HEAD_DIM)
        acc[:rows, at] = (
            g_buf[stage, :rows, g_at].astype(F32)
            + d_query[0]
            + both[0][2 * rows :]
            + both[1][rows : 2 * rows]
        )
        acc[rows:, at] = (
            g_buf[stage, rows:, g_at].astype(F32) + d_query[1] + both[1][2 * rows :]
        )

    def halo_wait(stage, h):
        @pl.when(h % X_HEADS == 0)
        def _():
            halo_copy(stage, h // X_HEADS).wait_recv()

    @pl.when(lower)
    def _():
        forward(1)

        def ahead(n, carry):
            halo_wait(n // heads, n % heads)
            prepare_head(n // heads, n % heads)
            return carry

        lax.fori_loop(0, 2 * heads, ahead, 0)

    def run_stage(stage, carry):
        @pl.when(stage == 0)
        def _():
            @pl.when(upper)
            def _():
                for f in range(g_chunks):
                    top_copy(f, 1 - side).wait_recv()
                    top_swap_copy(f, core).start()
                for f in range(g_chunks):
                    top_swap_copy(f, 1 - core).wait_recv()
                top_local().wait()

            @pl.when(lower)
            def _():
                for f in range(g_chunks):
                    down_copy(f).wait_recv()
                    swap_copy(0, f, core).start()
                for f in range(g_chunks):
                    swap_copy(0, f, 1 - core).wait_recv()

        @pl.when(stage == 1)
        def _():
            for f in range(g_chunks):
                swap_copy(1, f, 1 - core).wait_recv()

        w_arrival(stage).wait()

        def project(n, carry):
            at = cols(n, g_width)
            hg_buf[:, at] = dot_nt(g_buf[stage], w_buf[stage, at, :]).astype(BF16)
            return carry

        lax.fori_loop(0, g_chunks, project, 0)

        def attend(h, carry):
            @pl.when(upper)
            def _():
                halo_wait(stage, h)
                prepare_head(stage, h)

            attend_head(stage, h)
            con_copy(stage, h).start()

            @pl.when(upper & (stage == 0) & (h == heads // 2))
            def _():
                forward(1)

            return carry

        lax.fori_loop(0, heads, attend, 0)

        def finish(f, carry):
            for j in range(G_HEADS):
                con_copy(stage, f * G_HEADS + j).wait_recv()
            at = cols(f, g_width)
            total = acc[:, at] + con_recv[stage, :, at].astype(F32)
            g_buf[stage + 1, :, cols(core * g_chunks + f, g_width)] = total.astype(BF16)

            @pl.when(stage == 0)
            def _():
                swap_copy(1, f, core).start()

            @pl.when((stage == 1) & upper)
            def _():
                down_copy(f).start()

            @pl.when(core + stage == 1)
            def _():
                out_local(stage, f).start()

            @pl.when(core + stage != 1)
            def _():
                out_partner(stage, f).start()

            out_beside(stage, f).start()
            return carry

        lax.fori_loop(0, g_chunks, finish, 0)
        return carry

    lax.fori_loop(0, 2, run_stage, 0)

    gain_remote().wait_send()
    w_remote().wait_send()
    for i in range(x_chunks):
        for way in range(3):
            x_remote(i, way).wait_send()
        for stage in range(2):
            halo_copy(stage, i).wait_send()
    for f in range(g_chunks):
        swap_copy(1, f, core).wait_send()

        @pl.when(upper)
        def _():
            top_swap_copy(f, core).wait_send()
            down_copy(f).wait_send()

        @pl.when(lower)
        def _():
            swap_copy(0, f, core).wait_send()
            top_copy(f, side).wait_send()

        for stage in range(2):

            @pl.when(core + stage != 1)
            def _():
                out_partner(stage, f).wait_send()

            out_beside(stage, f).wait_send()
    for stage in range(2):
        for h in range(heads):
            con_copy(stage, h).wait_send()
    for micro in range(2):
        for core_at in range(2):
            for f in range(g_chunks):
                out_arrival(micro, core_at, f).wait()


def solution(mesh):
    pair_count = mesh.shape["ctx"] // 2

    def on_device(saved_inputs, scale_gains, out_proj, top_grad):
        _, micros, rows, features = saved_inputs.shape
        half_width = features // 2
        heads = half_width // HEAD_DIM
        x_chunks = heads // X_HEADS
        g_chunks = heads // G_HEADS
        dma = pltpu.SemaphoreType.DMA
        anywhere = pl.BlockSpec(memory_space=pl.ANY)
        result = pl.pallas_call(
            functools.partial(cascade_kernel, pair_count),
            out_shape=jax.ShapeDtypeStruct((micros, rows, features), BF16),
            in_specs=[anywhere] * 4,
            out_specs=anywhere,
            scratch_shapes=[
                pltpu.VMEM((2, 2 * rows, half_width), BF16),
                pltpu.VMEM((2, 2 * rows, half_width), BF16),
                pltpu.VMEM((2, 3, 1, half_width), F32),
                pltpu.VMEM((2, half_width, features), BF16),
                pltpu.VMEM((3, 2 * rows, features), BF16),
                pltpu.VMEM((2, heads, 4 * rows, HEAD_DIM), BF16),
                pltpu.VMEM((2, heads, 4 * rows, HEAD_DIM), BF16),
                pltpu.VMEM((2, heads, 2 * rows, HEAD_DIM), BF16),
                pltpu.VMEM((2, 2 * rows, half_width), F32),
                pltpu.VMEM((2, heads, 2, 2, rows, rows), F32),
                pltpu.VMEM((2, heads, 2, 3 * rows, rows), BF16),
                pltpu.VMEM((2 * rows, half_width), BF16),
                pltpu.VMEM((2 * rows, half_width), F32),
                pltpu.VMEM((2, 2 * rows, half_width), BF16),
                pltpu.VMEM((2, 2 * rows, half_width), BF16),
                dma,
                dma((2,)),
                dma,
                dma((2,)),
                dma,
                dma((3, x_chunks)),
                dma((2, 2, x_chunks)),
                dma((2, x_chunks)),
                dma((2, x_chunks)),
                dma((2, heads)),
                dma((2, heads)),
                dma((2, g_chunks)),
                dma((2, g_chunks)),
                dma((g_chunks,)),
                dma((g_chunks,)),
                dma((2, 2, g_chunks)),
                dma((2, 2, g_chunks)),
            ],
            compiler_params=pltpu.CompilerParams(collective_id=0, has_side_effects=True),
        )(saved_inputs[0], scale_gains.reshape(3, 1, features), out_proj[0], top_grad)
        return result[None]

    return jax.shard_map(
        on_device,
        mesh=mesh,
        in_specs=(
            P("segment", None, "ctx", None),
            P("segment", None, None),
            P("segment", None, None),
            P(None, "ctx", None),
        ),
        out_specs=P("segment", None, "ctx", None),
        check_vma=False,
    )
```

time: 696 us -> 101 us (0.15)
  the two profiles are of different devices: /device:TPU:15 before, /device:TPU:44 now
where the time goes in v1:
time: 101 us
  Pallas kernels  99 us (98%)
  local copies, waits for them, and re-layouts  2.3 us (2%)
    pallas_call x1, Pallas kernels, on_device(): pl.pallas_call(functools.partial(cascade_kernel, pair_count), out_shape=j...  99 us
    unnamed x1, local copies, waits for them, and re-layouts  2.3 us

profile of v1, /device:TPU:44, one launch (start us, length us, event | category | flops | bytes accessed | tf_op | source)
XLA Modules:
  0.0 101.3 jit_solution(12048104167651344626)
XLA Ops:
  0.0 99.0 %shard_map.46 = bf16[2,128,2048]{2,1,0:T(8,128)(2,1)} custom-call(bf16[2,128,2048]{2,1,0:T(8,128)(2,1)} %bitcast.6, f32[3,1,2048]{2,1,0:T(1,128)} %bitcast.7, bf16[2048,2048]{1,0:T(8,128)(2,1)} %bitcast.4, bf16[2,128,2048]{2,1,0:T(8,128)(2,1)} %top_hbm.1), custom_call_target="tpu_custom_call" | custom-call | tf_op jit(solution)/shard_map/pallas_call | solution.py:528
  99.0 2.3 %copy.6 = bf16[1,2,128,2048]{3,2,1,0:T(8,128)(2,1)} copy(bf16[1,2,128,2048]{3,2,1,0:T(8,128)(2,1)} %bitcast.5) | data formatting | bytes 2097152

commit v2 on v1

--- a/solution.py
+++ b/solution.py
@@ -8,7 +8,7 @@
 from jax.sharding import PartitionSpec as P
 
 HEAD_DIM = 128
-X_HEADS = 2
+X_HEADS = 1
 G_HEADS = 2
 QUERY_SCALE = 1.0 / 12.0
 SOFT_CAP = 50.0
@@ -48,7 +48,7 @@
     o_all,
     slopes,
     weight_t,
-    hg_buf,
+    hg_sum,
     acc,
     con_send,
     con_recv,
@@ -89,14 +89,16 @@
     lower = half == 0
     mine = jnp.where(upper, side, 1 - side)
     held = 1 - core
+    has_later = pair < pair_count - 1
+    has_earlier = pair > 0
 
     def place(half_at, core_at, pair_at, side_at):
         return (2 * half_at + core_at, 2 * pair_at + side_at)
 
     partner = place(half, 1 - core, pair, side)
     facing = place(1 - half, core, pair, 1 - side)
-    later = place(half, core, lax.rem(pair + 1, pair_count), side)
-    earlier = place(half, core, lax.rem(pair + pair_count - 1, pair_count), side)
+    later = place(half, core, jnp.minimum(pair + 1, pair_count - 1), side)
+    earlier = place(half, core, jnp.maximum(pair - 1, 0), side)
     beside = place(half, core, pair, 1 - side)
     across = place(half, 1 - core, pair, 1 - side)
 
@@ -196,27 +198,27 @@
             earlier,
         )
 
-    def swap_copy(stage, f, core_at):
-        ref = g_buf.at[stage, :, cols(core_at * g_chunks + f, g_width)]
-        return remote(ref, ref, swap_send_sem.at[stage, f], swap_sem.at[stage, f], partner)
-
-    def top_swap_copy(f, core_at):
-        ref = g_buf.at[0, cols(1 - side, rows), cols(core_at * g_chunks + f, g_width)]
-        return remote(ref, ref, swap_send_sem.at[0, f], swap_sem.at[0, f], partner)
-
-    def down_copy(f):
-        at = cols(core * g_chunks + f, g_width)
-        return remote(
-            g_buf.at[2, :, at], g_buf.at[0, :, at], cross_send_sem.at[f], cross_sem.at[f], facing
-        )
-
-    def top_copy(f, block):
-        at = cols(core * g_chunks + f, g_width)
+    def swap_copy(stage, h, core_at):
+        ref = g_buf.at[stage, :, cols(core_at * heads + h, HEAD_DIM)]
+        return remote(ref, ref, swap_send_sem.at[stage, h], swap_sem.at[stage, h], partner)
+
+    def top_swap_copy(h, core_at):
+        ref = g_buf.at[0, cols(1 - side, rows), cols(core_at * heads + h, HEAD_DIM)]
+        return remote(ref, ref, swap_send_sem.at[0, h], swap_sem.at[0, h], partner)
+
+    def down_copy(h):
+        at = cols(core * heads + h, HEAD_DIM)
+        return remote(
+            g_buf.at[2, :, at], g_buf.at[0, :, at], cross_send_sem.at[h], cross_sem.at[h], facing
+        )
+
+    def top_copy(h, block):
+        at = cols(core * heads + h, HEAD_DIM)
         return remote(
             top_hbm.at[mine, :, at],
             g_buf.at[0, cols(block, rows), at],
-            cross_send_sem.at[f],
-            cross_sem.at[f],
+            cross_send_sem.at[h],
+            cross_sem.at[h],
             facing,
         )
 
@@ -260,10 +262,27 @@
         top_local().start()
 
     barrier = pltpu.get_barrier_semaphore()
-    peers = (partner, facing, later, earlier, beside, across)
-    for peer in peers:
+    for peer in (partner, facing, beside, across):
         pl.semaphore_signal(barrier, inc=1, device_id=peer, device_id_type=MESH)
-    pl.semaphore_wait(barrier, len(peers))
+
+    @pl.when(has_later)
+    def _():
+        pl.semaphore_signal(barrier, inc=1, device_id=later, device_id_type=MESH)
+
+    @pl.when(has_earlier)
+    def _():
+        pl.semaphore_signal(barrier, inc=1, device_id=earlier, device_id_type=MESH)
+
+    @pl.when(jnp.logical_not(has_earlier))
+    def _():
+        x_halo[...] = jnp.zeros_like(x_halo)
+
+    @pl.when(jnp.logical_not(has_later))
+    def _():
+        con_recv[...] = jnp.zeros_like(con_recv)
+
+    peers = 4 + has_later.astype(jnp.int32) + has_earlier.astype(jnp.int32)
+    pl.semaphore_wait(barrier, peers)
 
     def deliver():
         for i in range(x_chunks):
@@ -278,8 +297,8 @@
 
     @pl.when(lower)
     def _():
-        for f in range(g_chunks):
-            top_copy(f, side).start()
+        for h in range(heads):
+            top_copy(h, side).start()
 
     w_remote().start()
 
@@ -287,7 +306,10 @@
         for i in range(x_chunks):
             for block in range(2):
                 x_arrival(stage, block, i).wait()
-            halo_copy(stage, i).start()
+
+            @pl.when(has_later)
+            def _():
+                halo_copy(stage, i).start()
 
     forward(0)
 
@@ -346,7 +368,7 @@
         d_query = []
         for block in range(2):
             low = block * rows
-            hg = hg_buf[low : low + rows, at]
+            hg = hg_sum[low : low + rows, at].astype(BF16)
             hg_f = hg.astype(F32)
             gw = dot_nt(hg, v_all[stage, h, low : low + 3 * rows])
             row_dot = jnp.sum(hg_f * o_all[stage, low : low + rows, at], axis=1, keepdims=True)
@@ -380,100 +402,138 @@
             g_buf[stage, rows:, g_at].astype(F32) + d_query[1] + both[1][2 * rows :]
         )
 
-    def halo_wait(stage, h):
-        @pl.when(h % X_HEADS == 0)
+    def ready_head(stage, h):
+        @pl.when(has_earlier)
         def _():
-            halo_copy(stage, h // X_HEADS).wait_recv()
+            halo_copy(stage, h).wait_recv()
+
+        prepare_head(stage, h)
+
+    def absorb(stage, k):
+        at = cols(k, g_width)
+        hg_sum[...] += dot_nt(g_buf[stage, :, at], w_buf[stage, :, at])
+
+    def absorb_partner(stage, f):
+        for j in range(G_HEADS):
+            swap_copy(stage, f * G_HEADS + j, 1 - core).wait_recv()
+        absorb(stage, (1 - core) * g_chunks + f)
 
     @pl.when(lower)
     def _():
         forward(1)
 
         def ahead(n, carry):
-            halo_wait(n // heads, n % heads)
-            prepare_head(n // heads, n % heads)
+            ready_head(n // heads, n % heads)
             return carry
 
         lax.fori_loop(0, 2 * heads, ahead, 0)
 
+    hg_sum[...] = jnp.zeros_like(hg_sum)
+    w_arrival(0).wait()
+
+    @pl.when(upper)
+    def _():
+        top_local().wait()
+        for h in range(heads):
+            top_copy(h, 1 - side).wait_recv()
+            top_swap_copy(h, core).start()
+
+        def take(f, carry):
+            absorb(0, core * g_chunks + f)
+            for j in range(G_HEADS):
+                top_swap_copy(f * G_HEADS + j, 1 - core).wait_recv()
+            absorb(0, (1 - core) * g_chunks + f)
+            return carry
+
+        lax.fori_loop(0, g_chunks, take, 0)
+        ready_head(0, 0)
+
+    @pl.when(lower)
+    def _():
+        def take(f, carry):
+            @pl.when(f < g_chunks)
+            def _():
+                for j in range(G_HEADS):
+                    down_copy(f * G_HEADS + j).wait_recv()
+                    swap_copy(0, f * G_HEADS + j, core).start()
+                absorb(0, core * g_chunks + f)
+
+            @pl.when(f > 0)
+            def _():
+                absorb_partner(0, f - 1)
+
+            return carry
+
+        lax.fori_loop(0, g_chunks + 1, take, 0)
+
     def run_stage(stage, carry):
+        def attend(h, carry):
+            attend_head(stage, h)
+
+            @pl.when(has_earlier)
+            def _():
+                con_copy(stage, h).start()
+
+            @pl.when(upper & (stage == 0) & (h == 2))
+            def _():
+                forward(1)
+
+            @pl.when(upper & (stage * heads + h < 2 * heads - 1))
+            def _():
+                ready_head(stage + (h + 1) // heads, (h + 1) % heads)
+
+            return carry
+
+        lax.fori_loop(0, heads, attend, 0)
+
         @pl.when(stage == 0)
         def _():
-            @pl.when(upper)
-            def _():
-                for f in range(g_chunks):
-                    top_copy(f, 1 - side).wait_recv()
-                    top_swap_copy(f, core).start()
-                for f in range(g_chunks):
-                    top_swap_copy(f, 1 - core).wait_recv()
-                top_local().wait()
-
-            @pl.when(lower)
-            def _():
-                for f in range(g_chunks):
-                    down_copy(f).wait_recv()
-                    swap_copy(0, f, core).start()
-                for f in range(g_chunks):
-                    swap_copy(0, f, 1 - core).wait_recv()
-
-        @pl.when(stage == 1)
-        def _():
-            for f in range(g_chunks):
-                swap_copy(1, f, 1 - core).wait_recv()
-
-        w_arrival(stage).wait()
-
-        def project(n, carry):
-            at = cols(n, g_width)
-            hg_buf[:, at] = dot_nt(g_buf[stage], w_buf[stage, at, :]).astype(BF16)
+            hg_sum[...] = jnp.zeros_like(hg_sum)
+            w_arrival(1).wait()
+
+        def finish(f, carry):
+            @pl.when(f < g_chunks)
+            def _():
+                for j in range(G_HEADS):
+                    h = f * G_HEADS + j
+
+                    @pl.when(has_later)
+                    def _():
+                        con_copy(stage, h).wait_recv()
+
+                    at = cols(h, HEAD_DIM)
+                    total = acc[:, at] + con_recv[stage, :, at].astype(F32)
+                    g_buf[stage + 1, :, cols(core * heads + h, HEAD_DIM)] = total.astype(BF16)
+
+                    @pl.when(stage == 0)
+                    def _():
+                        swap_copy(1, h, core).start()
+
+                    @pl.when((stage == 1) & upper)
+                    def _():
+                        down_copy(h).start()
+
+                out_beside(stage, f).start()
+
+                @pl.when(core + stage == 1)
+                def _():
+                    out_local(stage, f).start()
+
+                @pl.when(core + stage != 1)
+                def _():
+                    out_partner(stage, f).start()
+
+                @pl.when(stage == 0)
+                def _():
+                    absorb(1, core * g_chunks + f)
+
+            @pl.when((stage == 0) & (f > 0))
+            def _():
+                absorb_partner(1, f - 1)
+
             return carry
 
-        lax.fori_loop(0, g_chunks, project, 0)
-
-        def attend(h, carry):
-            @pl.when(upper)
-            def _():
-                halo_wait(stage, h)
-                prepare_head(stage, h)
-
-            attend_head(stage, h)
-            con_copy(stage, h).start()
-
-            @pl.when(upper & (stage == 0) & (h == heads // 2))
-            def _():
-                forward(1)
-
-            return carry
-
-        lax.fori_loop(0, heads, attend, 0)
-
-        def finish(f, carry):
-            for j in range(G_HEADS):
-                con_copy(stage, f * G_HEADS + j).wait_recv()
-            at = cols(f, g_width)
-            total = acc[:, at] + con_recv[stage, :, at].astype(F32)
-            g_buf[stage + 1, :, cols(core * g_chunks + f, g_width)] = total.astype(BF16)
-
-            @pl.when(stage == 0)
-            def _():
-                swap_copy(1, f, core).start()
-
-            @pl.when((stage == 1) & upper)
-            def _():
-                down_copy(f).start()
-
-            @pl.when(core + stage == 1)
-            def _():
-                out_local(stage, f).start()
-
-            @pl.when(core + stage != 1)
-            def _():
-                out_partner(stage, f).start()
-
-            out_beside(stage, f).start()
-            return carry
-
-        lax.fori_loop(0, g_chunks, finish, 0)
+        lax.fori_loop(0, g_chunks + 1 - stage, finish, 0)
         return carry
 
     lax.fori_loop(0, 2, run_stage, 0)
@@ -483,31 +543,44 @@
     for i in range(x_chunks):
         for way in range(3):
             x_remote(i, way).wait_send()
+
+    @pl.when(has_later)
+    def _():
         for stage in range(2):
-            halo_copy(stage, i).wait_send()
-    for f in range(g_chunks):
-        swap_copy(1, f, core).wait_send()
-
-        @pl.when(upper)
+            for i in range(x_chunks):
+                halo_copy(stage, i).wait_send()
+
+    @pl.when(has_earlier)
+    def _():
+        for stage in range(2):
+            for h in range(heads):
+                con_copy(stage, h).wait_send()
+
+    for h in range(heads):
+        swap_copy(1, h, core).wait_send()
+
+    @pl.when(upper)
+    def _():
+        for h in range(heads):
+            top_swap_copy(h, core).wait_send()
+            down_copy(h).wait_send()
+
+    @pl.when(lower)
+    def _():
+        for h in range(heads):
+            swap_copy(0, h, core).wait_send()
+            top_copy(h, side).wait_send()
+
+    for stage in range(2):
+
+        @pl.when(core + stage != 1)
         def _():
-            top_swap_copy(f, core).wait_send()
-            down_copy(f).wait_send()
-
-        @pl.when(lower)
-        def _():
-            swap_copy(0, f, core).wait_send()
-            top_copy(f, side).wait_send()
-
-        for stage in range(2):
-
-            @pl.when(core + stage != 1)
-            def _():
+            for f in range(g_chunks):
                 out_partner(stage, f).wait_send()
 
+        for f in range(g_chunks):
             out_beside(stage, f).wait_send()
-    for stage in range(2):
-        for h in range(heads):
-            con_copy(stage, h).wait_send()
+
     for micro in range(2):
         for core_at in range(2):
             for f in range(g_chunks):
@@ -542,7 +615,7 @@
                 pltpu.VMEM((2, 2 * rows, half_width), F32),
                 pltpu.VMEM((2, heads, 2, 2, rows, rows), F32),
                 pltpu.VMEM((2, heads, 2, 3 * rows, rows), BF16),
-                pltpu.VMEM((2 * rows, half_width), BF16),
+                pltpu.VMEM((2 * rows, half_width), F32),
                 pltpu.VMEM((2 * rows, half_width), F32),
                 pltpu.VMEM((2, 2 * rows, half_width), BF16),
                 pltpu.VMEM((2, 2 * rows, half_width), BF16),
@@ -557,10 +630,10 @@
                 dma((2, x_chunks)),
                 dma((2, heads)),
                 dma((2, heads)),
-                dma((2, g_chunks)),
-                dma((2, g_chunks)),
-                dma((g_chunks,)),
-                dma((g_chunks,)),
+                dma((2, heads)),
+                dma((2, heads)),
+                dma((heads,)),
+                dma((heads,)),
                 dma((2, 2, g_chunks)),
                 dma((2, 2, g_chunks)),
             ],

time: 101 us -> 98.1 us (0.971); the launches traced: 101 us -> 97.4 us
  Pallas kernels: 99 us -> 95.1 us
    pallas_call x1, Pallas kernels: 99 us -> 95.1 us  [on_device(): pl.pallas_call(functools.partial(cascade_kernel, pair_count), out_shape=j...]
where the time goes in v2:
time: 98.1 us; the launch traced here: 97.4 us
  Pallas kernels  95.1 us (97%)
  local copies, waits for them, and re-layouts  2.3 us (2%)
    pallas_call x1, Pallas kernels, on_device(): pl.pallas_call(functools.partial(cascade_kernel, pair_count), out_shape=j...  95.1 us
    unnamed x1, local copies, waits for them, and re-layouts  2.3 us

profile of v2, /device:TPU:44, one launch (start us, length us, event | category | flops | bytes accessed | tf_op | source)
XLA Modules:
  0.0 97.4 jit_solution(7436731493461544454)
XLA Ops:
  0.0 95.1 %shard_map.46 = bf16[2,128,2048]{2,1,0:T(8,128)(2,1)} custom-call(bf16[2,128,2048]{2,1,0:T(8,128)(2,1)} %bitcast.6, f32[3,1,2048]{2,1,0:T(1,128)} %bitcast.7, bf16[2048,2048]{1,0:T(8,128)(2,1)} %bitcast.4, bf16[2,128,2048]{2,1,0:T(8,128)(2,1)} %top_hbm.1), custom_call_target="tpu_custom_call" | custom-call | tf_op jit(solution)/shard_map/pallas_call | solution.py:601
  95.1 2.3 %copy.6 = bf16[1,2,128,2048]{3,2,1,0:T(8,128)(2,1)} copy(bf16[1,2,128,2048]{3,2,1,0:T(8,128)(2,1)} %bitcast.5) | data formatting | bytes 2097152

commit v3 on v2

--- a/solution.py
+++ b/solution.py
@@ -222,34 +222,34 @@
             facing,
         )
 
-    def out_refs(stage, f, block):
-        at = cols(core * g_chunks + f, g_width)
+    def out_refs(stage, h, block):
+        at = cols(core * heads + h, HEAD_DIM)
         return g_buf.at[stage + 1, cols(block, rows), at], out_hbm.at[mine, :, at]
 
-    def out_local(stage, f):
-        src, dst = out_refs(stage, f, side)
-        return pltpu.make_async_copy(src, dst, out_sem.at[mine, core, f])
-
-    def out_partner(stage, f):
-        src, dst = out_refs(stage, f, side)
-        return remote(
-            src, dst, out_send_sem.at[stage, 0, f], out_sem.at[mine, core, f], partner
-        )
-
-    def out_beside(stage, f):
-        src, dst = out_refs(stage, f, 1 - side)
+    def out_local(stage, h):
+        src, dst = out_refs(stage, h, side)
+        return pltpu.make_async_copy(src, dst, out_sem.at[mine, core, h])
+
+    def out_partner(stage, h):
+        src, dst = out_refs(stage, h, side)
+        return remote(
+            src, dst, out_send_sem.at[stage, 0, h], out_sem.at[mine, core, h], partner
+        )
+
+    def out_beside(stage, h):
+        src, dst = out_refs(stage, h, 1 - side)
         return remote(
             src,
             dst,
-            out_send_sem.at[stage, 1, f],
-            out_sem.at[mine, core, f],
+            out_send_sem.at[stage, 1, h],
+            out_sem.at[mine, core, h],
             place(half, 1 - stage, pair, 1 - side),
         )
 
-    def out_arrival(micro, core_at, f):
-        at = cols(core_at * g_chunks + f, g_width)
-        return pltpu.make_async_copy(
-            g_buf.at[1, cols(0, rows), at], out_hbm.at[micro, :, at], out_sem.at[micro, core_at, f]
+    def out_arrival(micro, core_at, h):
+        at = cols(core_at * heads + h, HEAD_DIM)
+        return pltpu.make_async_copy(
+            g_buf.at[1, cols(0, rows), at], out_hbm.at[micro, :, at], out_sem.at[micro, core_at, h]
         )
 
     gain_local().start()
@@ -379,10 +379,7 @@
             d_cat = jnp.concatenate(
                 [jnp.where(own, 0.0, d_mix), d_one, jnp.where(own, d_mix, 0.0)], axis=1
             ).astype(BF16)
-            dt_mix = d_mix.T
-            d_t = jnp.concatenate(
-                [jnp.where(own_t, 0.0, dt_mix), d_one.T, jnp.where(own_t, dt_mix, 0.0)], axis=0
-            ).astype(BF16)
+            d_t = d_cat.T
             left = jnp.concatenate([d_t, weight_t[stage, h, block]], axis=1)
             right = jnp.concatenate(
                 [qg_all[stage, h, low : low + rows], (hg_f * gv).astype(BF16)], axis=0
@@ -467,24 +464,40 @@
         lax.fori_loop(0, g_chunks + 1, take, 0)
 
     def run_stage(stage, carry):
+        def send(h):
+            @pl.when(has_earlier)
+            def _():
+                con_copy(stage, h).start()
+
         def attend(h, carry):
             attend_head(stage, h)
-
+            send(h)
+            return carry
+
+        def attend_ahead(h, carry):
             @pl.when(has_earlier)
             def _():
-                con_copy(stage, h).start()
-
-            @pl.when(upper & (stage == 0) & (h == 2))
+                halo_copy(stage, h + 1).wait_recv()
+
+            attend_head(stage, h)
+            prepare_head(stage, h + 1)
+            send(h)
+
+            @pl.when((stage == 0) & (h == 2))
             def _():
                 forward(1)
 
-            @pl.when(upper & (stage * heads + h < 2 * heads - 1))
-            def _():
-                ready_head(stage + (h + 1) // heads, (h + 1) % heads)
-
             return carry
 
-        lax.fori_loop(0, heads, attend, 0)
+        @pl.when(upper)
+        def _():
+            lax.fori_loop(0, heads - 1, attend_ahead, 0)
+
+        lax.fori_loop(jnp.where(upper, heads - 1, 0), heads, attend, 0)
+
+        @pl.when(upper & (stage == 0))
+        def _():
+            ready_head(1, 0)
 
         @pl.when(stage == 0)
         def _():
@@ -513,15 +526,15 @@
                     def _():
                         down_copy(h).start()
 
-                out_beside(stage, f).start()
-
-                @pl.when(core + stage == 1)
-                def _():
-                    out_local(stage, f).start()
-
-                @pl.when(core + stage != 1)
-                def _():
-                    out_partner(stage, f).start()
+                    out_beside(stage, h).start()
+
+                    @pl.when(core + stage == 1)
+                    def _():
+                        out_local(stage, h).start()
+
+                    @pl.when(core + stage != 1)
+                    def _():
+                        out_partner(stage, h).start()
 
                 @pl.when(stage == 0)
                 def _():
@@ -575,16 +588,16 @@
 
         @pl.when(core + stage != 1)
         def _():
-            for f in range(g_chunks):
-                out_partner(stage, f).wait_send()
-
-        for f in range(g_chunks):
-            out_beside(stage, f).wait_send()
+            for h in range(heads):
+                out_partner(stage, h).wait_send()
+
+        for h in range(heads):
+            out_beside(stage, h).wait_send()
 
     for micro in range(2):
         for core_at in range(2):
-            for f in range(g_chunks):
-                out_arrival(micro, core_at, f).wait()
+            for h in range(heads):
+                out_arrival(micro, core_at, h).wait()
 
 
 def solution(mesh):
@@ -634,8 +647,8 @@
                 dma((2, heads)),
                 dma((heads,)),
                 dma((heads,)),
-                dma((2, 2, g_chunks)),
-                dma((2, 2, g_chunks)),
+                dma((2, 2, heads)),
+                dma((2, 2, heads)),
             ],
             compiler_params=pltpu.CompilerParams(collective_id=0, has_side_effects=True),
         )(saved_inputs[0], scale_gains.reshape(3, 1, features), out_proj[0], top_grad)

time: 98.1 us -> 95.9 us (0.978)
  Pallas kernels: 95.1 us -> 93.1 us
    pallas_call x1, Pallas kernels: 95.1 us -> 93.1 us  [on_device(): pl.pallas_call(functools.partial(cascade_kernel, pair_count), out_shape=j...]
where the time goes in v3:
time: 95.9 us; the launch traced here: 95.4 us
  Pallas kernels  93.1 us (97%)
  local copies, waits for them, and re-layouts  2.3 us (2%)
    pallas_call x1, Pallas kernels, on_device(): pl.pallas_call(functools.partial(cascade_kernel, pair_count), out_shape=j...  93.1 us
    unnamed x1, local copies, waits for them, and re-layouts  2.3 us

profile of v3, /device:TPU:44, one launch (start us, length us, event | category | flops | bytes accessed | tf_op | source)
XLA Modules:
  0.0 95.4 jit_solution(13305825379288777828)
XLA Ops:
  0.0 93.1 %shard_map.46 = bf16[2,128,2048]{2,1,0:T(8,128)(2,1)} custom-call(bf16[2,128,2048]{2,1,0:T(8,128)(2,1)} %bitcast.6, f32[3,1,2048]{2,1,0:T(1,128)} %bitcast.7, bf16[2048,2048]{1,0:T(8,128)(2,1)} %bitcast.4, bf16[2,128,2048]{2,1,0:T(8,128)(2,1)} %top_hbm.1), custom_call_target="tpu_custom_call" | custom-call | tf_op jit(solution)/shard_map/pallas_call | solution.py:614
  93.1 2.3 %copy.6 = bf16[1,2,128,2048]{3,2,1,0:T(8,128)(2,1)} copy(bf16[1,2,128,2048]{3,2,1,0:T(8,128)(2,1)} %bitcast.5) | data formatting | bytes 2097152

commit v4 on v3

--- a/solution.py
+++ b/solution.py
@@ -302,14 +302,17 @@
 
     w_remote().start()
 
+    def forward_one(stage, i):
+        for block in range(2):
+            x_arrival(stage, block, i).wait()
+
+        @pl.when(has_later)
+        def _():
+            halo_copy(stage, i).start()
+
     def forward(stage):
         for i in range(x_chunks):
-            for block in range(2):
-                x_arrival(stage, block, i).wait()
-
-            @pl.when(has_later)
-            def _():
-                halo_copy(stage, i).start()
+            forward_one(stage, i)
 
     forward(0)
 
@@ -483,9 +486,14 @@
             prepare_head(stage, h + 1)
             send(h)
 
-            @pl.when((stage == 0) & (h == 2))
-            def _():
-                forward(1)
+            @pl.when((stage == 0) & (h >= 0))
+            def _():
+                forward_one(1, h - 0)
+
+            @pl.when((stage == 0) & (h == heads - 2))
+            def _():
+                for i in range(x_chunks - 1, x_chunks):
+                    forward_one(1, i)
 
             return carry
 

time: 95.9 us -> 95.5 us (level)
  no operation moved by 1% of the time
where the time goes in v4:
time: 95.5 us; the launch traced here: 95.4 us
  Pallas kernels  93.1 us (97%)
  local copies, waits for them, and re-layouts  2.3 us (2%)
    pallas_call x1, Pallas kernels, on_device(): pl.pallas_call(functools.partial(cascade_kernel, pair_count), out_shape=j...  93.1 us
    unnamed x1, local copies, waits for them, and re-layouts  2.3 us

profile of v4, /device:TPU:44, one launch (start us, length us, event | category | flops | bytes accessed | tf_op | source)
XLA Modules:
  0.0 95.4 jit_solution(15650666808702076656)
XLA Ops:
  0.0 93.1 %shard_map.46 = bf16[2,128,2048]{2,1,0:T(8,128)(2,1)} custom-call(bf16[2,128,2048]{2,1,0:T(8,128)(2,1)} %bitcast.6, f32[3,1,2048]{2,1,0:T(1,128)} %bitcast.7, bf16[2048,2048]{1,0:T(8,128)(2,1)} %bitcast.4, bf16[2,128,2048]{2,1,0:T(8,128)(2,1)} %top_hbm.1), custom_call_target="tpu_custom_call" | custom-call | tf_op jit(solution)/shard_map/pallas_call | solution.py:622
  93.1 2.3 %copy.6 = bf16[1,2,128,2048]{3,2,1,0:T(8,128)(2,1)} copy(bf16[1,2,128,2048]{3,2,1,0:T(8,128)(2,1)} %bitcast.5) | data formatting | bytes 2097152

commit v5 on v4

--- a/solution.py
+++ b/solution.py
@@ -326,7 +326,6 @@
     row_at = lax.broadcasted_iota(jnp.int32, (rows, rows), 0)
     col_at = lax.broadcasted_iota(jnp.int32, (rows, rows), 1)
     own = col_at <= row_at
-    own_t = row_at <= col_at
     seen = (pair >= 1).astype(F32)
 
     def prepare_head(stage, h):
@@ -359,10 +358,7 @@
                 [jnp.where(own, 0.0, w_mix), w_one, jnp.where(own, w_mix, 0.0)], axis=1
             ).astype(BF16)
             o_all[stage, low : low + rows, at] = dot_nn(w_cat, v[span])
-            wt_mix = w_mix.T
-            weight_t[stage, h, block] = jnp.concatenate(
-                [jnp.where(own_t, 0.0, wt_mix), w_one.T, jnp.where(own_t, wt_mix, 0.0)], axis=0
-            ).astype(BF16)
+            weight_t[stage, h, block] = w_cat.T
 
     def attend_head(stage, h):
         at = cols(h, HEAD_DIM)

time: 95.5 us -> 95.6 us (level)
  no operation moved by 1% of the time
where the time goes in v5:
time: 95.6 us; the launch traced here: 95.5 us
  Pallas kernels  93.1 us (97%)
  local copies, waits for them, and re-layouts  2.3 us (2%)
    pallas_call x1, Pallas kernels, on_device(): pl.pallas_call(functools.partial(cascade_kernel, pair_count), out_shape=j...  93.1 us
    unnamed x1, local copies, waits for them, and re-layouts  2.3 us

profile of v5, /device:TPU:44, one launch (start us, length us, event | category | flops | bytes accessed | tf_op | source)
XLA Modules:
  0.0 95.5 jit_solution(6941766996371346277)
XLA Ops:
  0.0 93.1 %shard_map.46 = bf16[2,128,2048]{2,1,0:T(8,128)(2,1)} custom-call(bf16[2,128,2048]{2,1,0:T(8,128)(2,1)} %bitcast.6, f32[3,1,2048]{2,1,0:T(1,128)} %bitcast.7, bf16[2048,2048]{1,0:T(8,128)(2,1)} %bitcast.4, bf16[2,128,2048]{2,1,0:T(8,128)(2,1)} %top_hbm.1), custom_call_target="tpu_custom_call" | custom-call | tf_op jit(solution)/shard_map/pallas_call | solution.py:618
  93.1 2.3 %copy.6 = bf16[1,2,128,2048]{3,2,1,0:T(8,128)(2,1)} copy(bf16[1,2,128,2048]{3,2,1,0:T(8,128)(2,1)} %bitcast.5) | data formatting | bytes 2097152

commit v6 on v5

--- a/solution.py
+++ b/solution.py
@@ -602,6 +602,27 @@
         for core_at in range(2):
             for h in range(heads):
                 out_arrival(micro, core_at, h).wait()
+
+
+def hand_on_kernel(parts, in_hbm, out_hbm, held, in_sem, out_sem):
+    rows = in_hbm.shape[1] // (parts // 2)
+
+    def piece(ref, n):
+        return ref.at[n // (parts // 2), pl.ds((n % (parts // 2)) * rows, rows), :]
+
+    def load(n):
+        return pltpu.make_async_copy(piece(in_hbm, n), held.at[n], in_sem.at[n])
+
+    def store(n):
+        return pltpu.make_async_copy(held.at[n], piece(out_hbm, n), out_sem.at[n])
+
+    for n in range(parts):
+        load(n).start()
+    for n in range(parts):
+        load(n).wait()
+        store(n).start()
+    for n in range(parts):
+        store(n).wait()
 
 
 def solution(mesh):
@@ -656,6 +677,18 @@
             ],
             compiler_params=pltpu.CompilerParams(collective_id=0, has_side_effects=True),
         )(saved_inputs[0], scale_gains.reshape(3, 1, features), out_proj[0], top_grad)
+        parts = 8
+        result = pl.pallas_call(
+            functools.partial(hand_on_kernel, parts),
+            out_shape=jax.ShapeDtypeStruct(result.shape, BF16),
+            in_specs=[anywhere],
+            out_specs=anywhere,
+            scratch_shapes=[
+                pltpu.VMEM((parts, micros * rows // parts, features), BF16),
+                dma((parts,)),
+                dma((parts,)),
+            ],
+        )(result)
         return result[None]
 
     return jax.shard_map(

time: 95.6 us -> 95.3 us (level)
  local copies, waits for them, and re-layouts: 2.3 us -> 0 us
  Pallas kernels: 93.1 us -> 95.2 us
    unnamed x1 -> x0, local copies, waits for them, and re-layouts: 2.3 us -> none
    pallas_call x0 -> x1, Pallas kernels: none -> 2.09 us  [on_device(): pl.pallas_call(functools.partial(hand_on_kernel, parts), out_shape=jax.Sh...]
where the time goes in v6:
time: 95.3 us; the launch traced here: 95.2 us
  Pallas kernels  95.2 us (100%)
    pallas_call x1, Pallas kernels, on_device(): pl.pallas_call(functools.partial(cascade_kernel, pair_count), out_shape=j...  93.1 us
    pallas_call x1, Pallas kernels, on_device(): pl.pallas_call(functools.partial(hand_on_kernel, parts), out_shape=jax.Sh...  2.09 us

profile of v6, /device:TPU:44, one launch (start us, length us, event | category | flops | bytes accessed | tf_op | source)
XLA Modules:
  0.0 95.2 jit_solution(8141994577079139335)
XLA Ops:
  0.0 93.1 %shard_map.46.in_hbm = bf16[2,128,2048]{2,1,0:T(8,128)(2,1)} custom-call(bf16[2,128,2048]{2,1,0:T(8,128)(2,1)} %bitcast.5, f32[3,1,2048]{2,1,0:T(1,128)} %bitcast.6, bf16[2048,2048]{1,0:T(8,128)(2,1)} %bitcast.4, bf16[2,128,2048]{2,1,0:T(8,128)(2,1)} %top_hbm.1), custom_call_target="tpu_custom_call" | custom-call | tf_op jit(solution)/shard_map/pallas_call | solution.py:639
  93.1 2.1 %shard_map.47 = bf16[2,128,2048]{2,1,0:T(8,128)(2,1)} custom-call(bf16[2,128,2048]{2,1,0:T(8,128)(2,1)} %shard_map.46.in_hbm), custom_call_target="tpu_custom_call" | custom-call | tf_op jit(solution)/shard_map/pallas_call | solution.py:681
